TPU v7x, 512 devices: a whole 4x8x8 slice. The times are simulated.
512 devices in a mesh: row: 16 (over z, core), col: 32 (over x, y).
Axes of the slice: x: 4, y: 8, z: 8, core: 2. Of those that a mesh axis runs over, the one named last changes fastest.
Arguments:
- panel: bfloat16 [64, 1024, 256], P('row', 'col'), may hold values from -6 to 6
- inverse_factor: bfloat16 [1024, 1024], P('row', 'col'), as said below
- ranks: int32 [64], replicated, may hold values from 32 to 256
Outputs:
- solved: bfloat16 [64, 1024, 256], P('row', 'col')
- core_blocks: bfloat16 [64, 64, 256, 256], P('row', 'col')
Inputs may be any that keep to these rules, and one draw needn't show every extreme that they name: inverse_factor is lower triangular with a diagonal between 0.5 and 3.
All inputs are finite; a program needn't handle non-finite values.
Results may differ from a plain program's by a relative error of at most 0.017.
Values may be sent and summed in bfloat16 or wider, within the bound.
No kernel may reach another device: no remote copies, remote signals or barrier semaphores. Data moves between devices by JAX's collectives and lax.ppermute only.
A program may use at most 64 MiB of HBM per device.

v0:
```python
import jax
import jax.numpy as jnp
from jax import lax
from jax.sharding import PartitionSpec as P


def sent_to_all(value, axis):
    copies = jnp.broadcast_to(value, (lax.axis_size(axis), *value.shape))
    return lax.all_to_all(copies, axis, split_axis=0, concat_axis=0, tiled=True)


def joined_along(pieces, dim):
    shape = list(pieces.shape[1:])
    shape[dim] *= pieces.shape[0]
    return jnp.moveaxis(pieces, 0, dim).reshape(shape)


def collect(value, axis, dim):
    pieces = sent_to_all(value, axis)
    return joined_along(pieces, dim)


def in_blocks(value, dim, count):
    shape = value.shape
    pieces = value.reshape(*shape[:dim], count, shape[dim] // count, *shape[dim + 1 :])
    return jnp.moveaxis(pieces, dim, 0)


def sent_and_summed(value, axis, dim):
    count = lax.axis_size(axis)
    pieces = lax.all_to_all(in_blocks(value, dim, count), axis, 0, 0, tiled=True)
    return jnp.sum(pieces.astype(jnp.float32), axis=0)


def from_root(value, axis, root):
    return lax.dynamic_index_in_dim(lax.all_gather(value, axis), root, 0, keepdims=False)


def per_device(panel, inverse_factor, ranks):
    tile_count = panel.shape[0]
    rank_width = panel.shape[2]
    row_index = lax.axis_index("row")
    col_index = lax.axis_index("col")
    col_count = lax.axis_size("col")
    row_count = lax.axis_size("row")
    factor_cols = collect(inverse_factor, "row", 0)
    own_ranks = lax.dynamic_slice_in_dim(ranks, row_index * tile_count, tile_count, 0)
    column_ids = jnp.arange(rank_width, dtype=jnp.int32)
    keep_cols = (column_ids[None, :] < own_ranks[:, None]).astype(jnp.bfloat16)
    masked = panel * keep_cols[:, None, :]
    partial_value = jnp.einsum(
        "ab,tbr->tar", factor_cols, masked, preferred_element_type=jnp.float32
    )
    shares = sent_and_summed(partial_value.astype(jnp.bfloat16), "col", 1).astype(jnp.bfloat16)
    solved_full = collect(shares, "col", 1)
    tiles_per_col = tile_count * row_count // col_count
    first_tile = col_index * tiles_per_col
    source = first_tile // tile_count
    offset = first_tile % tile_count
    picked = lax.dynamic_slice_in_dim(solved_full, offset, tiles_per_col, 0)
    col_tiles = from_root(picked, "row", source)
    core_blocks = jnp.einsum(
        "tar,uas->turs", solved_full, col_tiles, preferred_element_type=jnp.float32
    ).astype(jnp.bfloat16)
    return (shares, core_blocks)


def solution(mesh):
    return jax.shard_map(
        per_device,
        mesh=mesh,
        in_specs=(P("row", "col", None), P("row", "col"), P()),
        out_specs=(P("row", "col", None), P("row", "col", None, None)),
        check_vma=False,
    )
```

profile of v0, /device:TPU:1, one launch (start us, length us, event | category | flops | bytes accessed | tf_op | source)
XLA Modules:
  0.0 257.9 jit_solution(16094385965925276231)
XLA Ops:
  7.2 0.0 copy-start
  7.2 0.7 copy-done
  7.9 0.8 reshape.39
  8.7 11.8 %all-to-all-start = ((bf16[16,2,1024]{2,1,0:T(2,128)(2,1)}), bf16[16,2,1024]{2,1,0:T(2,128)(2,1)S(1)}, u32[]{:S(2)}, u32[]{:S(2)}) async-start(bf16[16,2,1024]{2,1,0:T(2,128)(2,1)} %reshape.39), calls=%async_computation | async-start | bytes 131072 | tf_op jit(solution)/shard_map/all_to_all | solution.py:9
  20.5 0.7 dynamic_slice.10
  21.2 0.1 fusion.5
  21.3 7.0 %all-to-all-done = bf16[16,2,1024]{2,1,0:T(2,128)(2,1)S(1)} async-done(((bf16[16,2,1024]{2,1,0:T(2,128)(2,1)}), bf16[16,2,1024]{2,1,0:T(2,128)(2,1)S(1)}, u32[]{:S(2)}, u32[]{:S(2)}) %all-to-all-start) | async-done | bytes 65568 | tf_op jit(solution)/shard_map/all_to_all | solution.py:9
  28.2 0.1 reshape.40
  28.4 0.1 copy.10
  28.5 0.1 reshape.35
  28.6 1.6 convert_bitcast_fusion
  30.2 2.6 copy.11
  32.8 1.8 copy.12
  34.5 57.2 %all_to_all.15 = bf16[32,4,32,256]{3,2,1,0:T(8,128)(2,1)S(1)} all-to-all(bf16[32,4,32,256]{3,2,1,0:T(8,128)(2,1)S(1)} %copy.12), channel_id=1, replica_groups=mesh['row'=16,'col'=32] {'col'}, dimensions={0} | all-to-all | bytes 4194304 | tf_op jit(solution)/shard_map/all_to_all | solution.py:31
  91.8 0.4 reduce_sum.12
  92.1 0.0 copy-start.2
  92.2 1.6 broadcast_in_dim.10
  93.8 0.0 copy-done.2
  93.8 8.2 %all-to-all-start.2 = ((bf16[32,4,32,256]{3,2,1,0:T(8,128)(2,1)}), bf16[32,4,32,256]{3,2,1,0:T(8,128)(2,1)S(1)}, u32[]{:S(2)}, u32[]{:S(2)}) async-start(bf16[32,4,32,256]{3,2,1,0:T(8,128)(2,1)} %broadcast_in_dim.10), calls=%async_computation.2 | async-start | bytes 4194304 | tf_op jit(solution)/shard_map/all_to_all | solution.py:9
  101.9 0.0 all-gather.3.cloned.1.call-start
  102.0 48.7 %all-to-all-done.2 = bf16[32,4,32,256]{3,2,1,0:T(8,128)(2,1)S(1)} async-done(((bf16[32,4,32,256]{3,2,1,0:T(8,128)(2,1)}), bf16[32,4,32,256]{3,2,1,0:T(8,128)(2,1)S(1)}, u32[]{:S(2)}, u32[]{:S(2)}) %all-to-all-start.2) | async-done | bytes 2097184 | tf_op jit(solution)/shard_map/all_to_all | solution.py:9
  150.7 0.2 copy.13
  150.8 0.0 copy-start.1
  150.9 1.3 copy-done.1
  152.2 1.0 constant_dynamic-slice_fusion
  153.2 0.0 all-gather.3.cloned.1.call-update
  153.3 93.3 %all-gather.3.cloned.1.call-done = bf16[32,1024,256]{2,1,0:T(8,128)(2,1)} async-done(((bf16[2,1024,256]{2,1,0:T(8,128)(2,1)}), bf16[32,1024,256]{2,1,0:T(8,128)(2,1)}) %all-gather.3.cloned.1.call-update) | async-done | bytes 16777232 | tf_op jit(solution)/shard_map/all_gather | solution.py:36
  246.6 3.2 %fusion = bf16[4,2,256,256]{2,3,0,1:T(8,128)(2,1)S(1)} fusion(bf16[4,1024,256,1]{2,1,0,3:T(8,128)(2,1)} %bitcast.29, bf16[16,2,1024,256]{3,2,1,0:T(8,128)(2,1)} %bitcast.31, s32[]{:T(128)S(6)} %select_n.25), kind=kOutput, calls=%fused_computation.2 | convolution fusion | flops 1074266112 | bytes 4194308 | tf_op jit(solution)/shard_map/tar,uas->turs/dot_general | solution.py:62
  249.7 1.3 copy.15
  (1 shorter events, 0.0 us)
Async XLA Ops:
  7.2 0.7 copy-start
  8.7 19.6 %all-to-all-start = ((bf16[16,2,1024]{2,1,0:T(2,128)(2,1)}), bf16[16,2,1024]{2,1,0:T(2,128)(2,1)S(1)}, u32[]{:S(2)}, u32[]{:S(2)}) async-start(bf16[16,2,1024]{2,1,0:T(2,128)(2,1)} %reshape.39), calls=%async_computation | async-start | bytes 131072 | tf_op jit(solution)/shard_map/all_to_all | solution.py:9
  92.1 1.6 copy-start.2
  93.8 56.9 %all-to-all-start.2 = ((bf16[32,4,32,256]{3,2,1,0:T(8,128)(2,1)}), bf16[32,4,32,256]{3,2,1,0:T(8,128)(2,1)S(1)}, u32[]{:S(2)}, u32[]{:S(2)}) async-start(bf16[32,4,32,256]{3,2,1,0:T(8,128)(2,1)} %broadcast_in_dim.10), calls=%async_computation.2 | async-start | bytes 4194304 | tf_op jit(solution)/shard_map/all_to_all | solution.py:9
  101.9 144.6 %all-gather.3.cloned.1.call-start = ((), (), s32[]{:S(2)}) async-start(), calls=%async_computation.3 | async-start | bytes 17825792 | tf_op jit(solution)/shard_map/all_gather | solution.py:36
  150.8 1.3 copy-start.1
Sparse Core Ops, SparseCore 0:
  153.4 93.1 all-gather.2
where the time goes:
time: 258 us
  waiting for transfers between devices  149 us (58%)
  blocking collectives  57.2 us (22%)
  starting transfers between devices  20 us (8%)
  between operations  14.1 us (5%)
  local copies, waits for them, and re-layouts  12.4 us (5%)
  matrix products  4.75 us (2%)
    all_gather x1, waiting for transfers between devices, from_root(): lax.all_gather(value, axis)  93.3 us
    all_to_all x1, blocking collectives, sent_and_summed(): lax.all_to_all(in_blocks(value, dim, count), axis, 0, 0, tiled=True)  57.2 us
    all_to_all x2, waiting for transfers between devices, sent_to_all(): return lax.all_to_all(copies, axis, split_axis=0, concat_axis=0, tiled=True)  55.6 us
    all_to_all x2, starting transfers between devices, sent_to_all(): return lax.all_to_all(copies, axis, split_axis=0, concat_axis=0, tiled=True)  20 us
  transfers between devices with their start and end apart: 3, of which 3 were waited for; matrix products, arithmetic and copies ran while one was open for 0% of the time, Pallas kernels for 0%

commit v1 on v0

v1 whole, which is shorter than its diff:
```python
import jax
import jax.numpy as jnp
from jax import lax
from jax.sharding import Mesh
from jax.sharding import PartitionSpec as P

ROW = ("z", "core")
COL = ("x", "y")
ALL = ROW + COL


def size_of(axes):
    axes = axes if isinstance(axes, tuple) else (axes,)
    count = 1
    for axis in axes:
        count *= lax.axis_size(axis)
    return count


def sent_to_all(value, axes):
    copies = jnp.broadcast_to(value, (size_of(axes), *value.shape))
    return lax.all_to_all(copies, axes, split_axis=0, concat_axis=0, tiled=True)


def kept(value, ranks):
    columns = jnp.arange(value.shape[-1], dtype=jnp.int32)
    return value * (columns[None, :] < ranks[:, None]).astype(value.dtype)[:, None, :]


def column_tiles(panel, col, rows, cols):
    odd = lax.rem(col, 2)
    pair = panel.shape[0] // 2

    def moved(flip):
        half = lax.bitwise_xor(odd, flip)
        part = lax.dynamic_slice_in_dim(panel, pair * half, pair, 0)
        pairs = [
            (r * cols + c, (c // 2) * cols + 2 * r + ((c % 2) ^ flip))
            for r in range(rows)
            for c in range(cols)
        ]
        return lax.ppermute(part, ALL, pairs)

    first, second = moved(0), moved(1)
    low = jnp.where(odd == 0, first, second)
    high = jnp.where(odd == 0, second, first)
    return jnp.concatenate([low, high], axis=1)


def per_device(panel, inverse_factor, ranks):
    tiles, depth, width = panel.shape
    core = lax.axis_index("core")
    row = lax.axis_index(ROW)
    col = lax.axis_index(COL)
    rows, cols = size_of(ROW), size_of(COL)
    pair = tiles * rows // cols

    part = column_tiles(panel, col, rows, cols)

    factor = lax.all_gather(inverse_factor.T, "core", axis=1, tiled=True)
    half = depth // 2
    lanes = factor.shape[1]
    factor = lax.dynamic_slice_in_dim(factor, half * core, half, 0)
    factor = sent_to_all(factor, COL)

    part_rows = part.shape[1]
    sides = width // lanes
    packed = jnp.concatenate(
        [
            factor.reshape(cols * half, lanes),
            jnp.moveaxis(part.reshape(pair, part_rows, sides, lanes), 2, 0).reshape(-1, lanes),
        ],
        axis=0,
    )
    packed = lax.all_gather(packed, ROW)
    count = cols * half
    whole = packed[:, :count].reshape(rows // 2, 2, cols, half, lanes)
    whole = whole.transpose(2, 1, 3, 0, 4).reshape(cols * depth, -1)
    mine = packed[:, count:].reshape(rows, sides, pair, part_rows, lanes)
    mine = mine.transpose(2, 0, 3, 1, 4).reshape(pair, rows * part_rows, width)

    full = sent_to_all(sent_to_all(panel, "y"), "x")
    full = full.reshape(cols, tiles, depth, width).transpose(1, 0, 2, 3)
    full = full.reshape(tiles, cols * depth, width)

    full = kept(full, lax.dynamic_slice_in_dim(ranks, row * tiles, tiles, 0))
    mine = kept(mine, lax.dynamic_slice_in_dim(ranks, col * pair, pair, 0))

    def solve(value):
        out = jnp.einsum("ba,tbr->tar", whole, value, preferred_element_type=jnp.float32)
        return out.astype(jnp.bfloat16)

    solved_full = solve(full)
    solved_mine = solve(mine)
    shares = lax.dynamic_slice_in_dim(solved_full, col * depth, depth, 1)
    core_blocks = jnp.einsum(
        "tar,uas->turs", solved_full, solved_mine, preferred_element_type=jnp.float32
    ).astype(jnp.bfloat16)
    return shares, core_blocks


def solution(mesh):
    split = Mesh(mesh.devices.reshape(8, 2, 4, 8), ALL)
    return jax.shard_map(
        per_device,
        mesh=split,
        in_specs=(P(ROW, COL, None), P(ROW, COL), P()),
        out_specs=(P(ROW, COL, None), P(ROW, COL, None, None)),
        check_vma=False,
    )
```

time: 258 us -> 130 us (0.50)
  the two profiles are of different devices: /device:TPU:1 before, /device:TPU:128 now
where the time goes in v1:
time: 130 us
  waiting for transfers between devices  34.4 us (26%)
  starting transfers between devices  27.7 us (21%)
  blocking collectives  22.4 us (17%)
  local copies, waits for them, and re-layouts  16.9 us (13%)
  between operations  14.2 us (11%)
  matrix products  10.4 us (8%)
  other arithmetic  3.59 us (3%)
    all_to_all x2, waiting for transfers between devices, sent_to_all(): return lax.all_to_all(copies, axes, split_axis=0, concat_axis=0, tiled=True)  34.4 us
    all_to_all x1, blocking collectives, sent_to_all(): return lax.all_to_all(copies, axes, split_axis=0, concat_axis=0, tiled=True)  19.4 us
    all_to_all x2, starting transfers between devices, sent_to_all(): return lax.all_to_all(copies, axes, split_axis=0, concat_axis=0, tiled=True)  19 us
    ppermute x2, starting transfers between devices, moved(): return lax.ppermute(part, ALL, pairs)  8.64 us
    dot_general x1, matrix products, solve(): jnp.einsum('ba,tbr->tar', whole, value, preferred_element_type=jnp.float32)  6.11 us
    dot_general x1, matrix products, per_device(): jnp.einsum('tar,uas->turs', solved_full, solved_mine, preferred_element_t...  4.27 us
    broadcast_in_dim x3, local copies, waits for them, and re-layouts, sent_to_all(): copies = jnp.broadcast_to(value, (size_of(axes), *value.shape))  3.21 us
    all_gather x1, blocking collectives, per_device(): factor = lax.all_gather(inverse_factor.T, 'core', axis=1, tiled=True)  3.04 us
  transfers between devices with their start and end apart: 5, of which 2 were waited for; matrix products, arithmetic and copies ran while one was open for 4% of the time, Pallas kernels for 0%

profile of v1, /device:TPU:128, one launch (start us, length us, event | category | flops | bytes accessed | tf_op | source)
XLA Modules:
  0.0 129.7 jit_solution(5983271142760320367)
XLA Ops:
  7.2 0.8 constant_dynamic-slice_fusion.1
  8.0 1.9 %collective-permute-start = (bf16[2,32,256]{2,1,0:T(8,128)(2,1)S(1)}, bf16[2,32,256]{2,1,0:T(8,128)(2,1)S(1)}, u32[]{:S(2)}, u32[]{:S(2)}) collective-permute-start(bf16[2,32,256]{2,1,0:T(8,128)(2,1)S(1)} %get-tuple-element.12), channel_id=1, source_target_pairs={{0,0},{1,1},{2,32},{3,33},{4,64},{5,65},{6,96},{7,97},{8,128},{9,1... | collective-permute-start | bytes 98312 | tf_op jit(solution)/shard_map/ppermute | solution.py:42
  9.9 6.7 %collective-permute-start.1 = (bf16[2,32,256]{2,1,0:T(8,128)(2,1)S(1)}, bf16[2,32,256]{2,1,0:T(8,128)(2,1)S(1)}, u32[]{:S(2)}, u32[]{:S(2)}) collective-permute-start(bf16[2,32,256]{2,1,0:T(8,128)(2,1)S(1)} %get-tuple-element.13), channel_id=1, source_target_pairs={{0,1},{1,0},{2,33},{3,32},{4,65},{5,64},{6,97},{7,96},{8,129},{9,1... | collective-permute-start | bytes 98312 | tf_op jit(solution)/shard_map/ppermute | solution.py:42
  16.6 3.0 %all-gather.1 = bf16[2,64,32]{1,2,0:T(8,128)(2,1)S(1)} all-gather(bf16[1,64,32]{1,2,0:T(8,128)(2,1)} %bitcast.55), channel_id=1, replica_groups=mesh['z'=8,'core'=2,'x'=4,'y'=8] {'core'}, dimensions={0}, use_global_device_ids=true | all-gather | bytes 12288 | tf_op jit(solution)/shard_map/all_gather | solution.py:60
  19.7 0.1 reshape.76
  19.8 0.7 broadcast_in_dim.8
  20.5 15.3 %all-to-all-start.2 = ((bf16[32,16,128]{2,1,0:T(8,128)(2,1)}), bf16[32,16,128]{2,1,0:T(8,128)(2,1)S(1)}, u32[]{:S(2)}, u32[]{:S(2)}) async-start(bf16[32,16,128]{2,1,0:T(8,128)(2,1)} %broadcast_in_dim.8), calls=%async_computation.2 | async-start | bytes 262144 | tf_op jit(solution)/shard_map/all_to_all | solution.py:22
  35.8 0.0 all-gather.4.cloned.1.call-start
  35.9 10.5 %all-to-all-done.2 = bf16[32,16,128]{2,1,0:T(8,128)(2,1)S(1)} async-done(((bf16[32,16,128]{2,1,0:T(8,128)(2,1)}), bf16[32,16,128]{2,1,0:T(8,128)(2,1)S(1)}, u32[]{:S(2)}, u32[]{:S(2)}) %all-to-all-start.2) | async-done | bytes 131104 | tf_op jit(solution)/shard_map/all_to_all | solution.py:22
  46.4 0.7 pad_maximum_fusion
  47.1 0.9 broadcast_in_dim.6
  48.0 19.4 %all_to_all.15 = bf16[8,4,32,256]{3,2,1,0:T(8,128)(2,1)S(1)} all-to-all(bf16[8,4,32,256]{3,2,1,0:T(8,128)(2,1)S(1)} %broadcast_in_dim.6), channel_id=1, replica_groups=mesh['z'=8,'core'=2,'x'=4,'y'=8] {'y'}, dimensions={0} | all-to-all | bytes 1048576 | tf_op jit(solution)/shard_map/all_to_all | solution.py:22
  67.4 1.6 %broadcast_in_dim.7 = bf16[4,8,4,32,256]{4,3,1,2,0:T(8,128)(2,1)} broadcast(bf16[8,4,32,256]{3,2,0,1:T(8,128)(2,1)S(1)} %copy.26), dimensions={1,2,3,4} | broadcast | bytes 2621440 | tf_op jit(solution)/shard_map/broadcast_in_dim | solution.py:21
  69.1 3.7 %all-to-all-start.1 = ((bf16[4,8,4,32,256]{4,3,1,2,0:T(8,128)(2,1)}), bf16[4,8,4,32,256]{4,3,1,2,0:T(8,128)(2,1)S(1)}, u32[]{:S(2)}, u32[]{:S(2)}) async-start(bf16[4,8,4,32,256]{4,3,1,2,0:T(8,128)(2,1)} %broadcast_in_dim.7), calls=%async_computation.1 | async-start | bytes 4194304 | tf_op jit(solution)/shard_map/all_to_all | solution.py:22
  72.9 0.1 dynamic_slice.23
  72.9 0.1 dynamic_slice.18
  73.0 0.1 fusion.9
  73.1 0.1 compare_convert_fusion
  73.2 23.9 %all-to-all-done.1 = bf16[4,8,4,32,256]{4,3,1,2,0:T(8,128)(2,1)S(1)} async-done(((bf16[4,8,4,32,256]{4,3,1,2,0:T(8,128)(2,1)}), bf16[4,8,4,32,256]{4,3,1,2,0:T(8,128)(2,1)S(1)}, u32[]{:S(2)}, u32[]{:S(2)}) %all-to-all-start.1) | async-done | bytes 2097184 | tf_op jit(solution)/shard_map/all_to_all | solution.py:22
  97.1 0.2 copy.27
  97.3 1.5 %broadcast_multiply_fusion = bf16[32,4,32,256]{3,2,0,1:T(8,128)(2,1)} fusion(bf16[32,4,32,256]{3,2,0,1:T(8,128)(2,1)S(1)} %bitcast.46, bf16[4,256]{1,0:T(4,128)(2,1)S(1)} %fusion.9), kind=kLoop, calls=%fused_computation.8 | loop fusion | flops 1048576 | bytes 4196352 | tf_op jit(solution)/shard_map/mul | solution.py:27
  98.8 1.3 slice.9
  100.1 1.8 %slice.8 = bf16[16,512,128]{2,1,0:T(8,128)(2,1)S(1)} slice(bf16[16,768,128]{2,1,0:T(8,128)(2,1)} %bitcast.50), slice={[0:16], [0:512], [0:128]} | slice | bytes 4194304 | tf_op jit(solution)/shard_map/slice | solution.py:77
  101.8 2.4 %copy.30 = bf16[32,2,16,8,128]{4,3,2,1,0:T(8,128)(2,1)S(1)} copy(bf16[32,2,16,8,128]{4,2,0,1,3:T(8,128)(2,1)S(1)} %bitcast.47) | data formatting | bytes 4194304 | tf_op jit(solution)/shard_map/transpose | solution.py:78
  104.3 2.3 %reshape.77 = bf16[1024,1024,1]{1,0,2:T(8,128)(2,1)} reshape(bf16[32,2,16,8,128]{4,3,2,1,0:T(8,128)(2,1)S(1)} %copy.30) | data formatting | bytes 4194304 | tf_op jit(solution)/shard_map/reshape | solution.py:78
  106.6 1.2 bitcast_multiply_fusion
  107.8 1.5 %mul.59 = bf16[2,1024,256]{2,1,0:T(8,128)(2,1)} reshape(bf16[2,16,64,2,128]{4,3,2,1,0:T(2,128)(2,1)S(1)} %bitcast_multiply_fusion) | data formatting | bytes 2097152 | tf_op jit(solution)/shard_map/mul | solution.py:27
  109.3 6.1 %convolution_convert_fusion = bf16[4,256,1024]{2,1,0:T(8,128)(2,1)} fusion(bf16[4,1024,256]{2,1,0:T(8,128)(2,1)} %bitcast.51, bf16[1024,1024,1]{1,0,2:T(8,128)(2,1)} %reshape.77), kind=kOutput, calls=%fused_computation.2 | convolution fusion | flops 2148532224 | bytes 6291456 | tf_op jit(solution)/shard_map/ba,tbr->tar/dot_general | solution.py:90
  115.4 4.3 %fusion.6 = bf16[4,2,256,256]{2,3,0,1:T(8,128)(2,1)S(1)} fusion(bf16[4,256,1024]{2,1,0:T(8,128)(2,1)} %convolution_convert_fusion, bf16[2,1024,256]{2,1,0:T(8,128)(2,1)} %mul.59, bf16[1024,1024,1]{1,0,2:T(8,128)(2,1)S(1)} %copy-done), kind=kOutput, calls=%fused_computation.6 | convolution fusion | flops 2148532224 | bytes 6291456 | tf_op jit(solution)/shard_map/tar,uas->turs/dot_general | solution.py:96
  119.7 1.1 dynamic-slice_bitcast_fusion
  120.8 0.8 copy.35
  121.6 1.3 %copy.36 = bf16[4,2,256,256]{3,2,1,0:T(8,128)(2,1)} copy(bf16[4,2,256,256]{2,3,0,1:T(8,128)(2,1)S(1)} %fusion.6) | data formatting | bytes 2097152
  (16 shorter events, 0.1 us)
Async XLA Ops:
  8.0 27.9 %collective-permute-start = (bf16[2,32,256]{2,1,0:T(8,128)(2,1)S(1)}, bf16[2,32,256]{2,1,0:T(8,128)(2,1)S(1)}, u32[]{:S(2)}, u32[]{:S(2)}) collective-permute-start(bf16[2,32,256]{2,1,0:T(8,128)(2,1)S(1)} %get-tuple-element.12), channel_id=1, source_target_pairs={{0,0},{1,1},{2,32},{3,33},{4,64},{5,65},{6,96},{7,97},{8,128},{9,1... | collective-permute-start | bytes 98312 | tf_op jit(solution)/shard_map/ppermute | solution.py:42
  9.9 25.9 %collective-permute-start.1 = (bf16[2,32,256]{2,1,0:T(8,128)(2,1)S(1)}, bf16[2,32,256]{2,1,0:T(8,128)(2,1)S(1)}, u32[]{:S(2)}, u32[]{:S(2)}) collective-permute-start(bf16[2,32,256]{2,1,0:T(8,128)(2,1)S(1)} %get-tuple-element.13), channel_id=1, source_target_pairs={{0,1},{1,0},{2,33},{3,32},{4,65},{5,64},{6,97},{7,96},{8,129},{9,1... | collective-permute-start | bytes 98312 | tf_op jit(solution)/shard_map/ppermute | solution.py:42
  20.5 25.9 %all-to-all-start.2 = ((bf16[32,16,128]{2,1,0:T(8,128)(2,1)}), bf16[32,16,128]{2,1,0:T(8,128)(2,1)S(1)}, u32[]{:S(2)}, u32[]{:S(2)}) async-start(bf16[32,16,128]{2,1,0:T(8,128)(2,1)} %broadcast_in_dim.8), calls=%async_computation.2 | async-start | bytes 262144 | tf_op jit(solution)/shard_map/all_to_all | solution.py:22
  35.8 63.0 %all-gather.4.cloned.1.call-start = ((), (), s32[]{:S(2)}) async-start(), calls=%async_computation.3 | async-start | bytes 3342336 | tf_op jit(solution)/shard_map/all_gather | solution.py:75
  69.1 3.8 %copy-start.1 = (s32[64]{0:T(128)S(1)}, s32[64]{0:T(128)}, u32[]{:S(2)}) copy-start(s32[64]{0:T(128)} %param.5) | copy-start | bytes 772
  69.1 28.0 %all-to-all-start.1 = ((bf16[4,8,4,32,256]{4,3,1,2,0:T(8,128)(2,1)}), bf16[4,8,4,32,256]{4,3,1,2,0:T(8,128)(2,1)S(1)}, u32[]{:S(2)}, u32[]{:S(2)}) async-start(bf16[4,8,4,32,256]{4,3,1,2,0:T(8,128)(2,1)} %broadcast_in_dim.7), calls=%async_computation.1 | async-start | bytes 4194304 | tf_op jit(solution)/shard_map/all_to_all | solution.py:22
  109.3 6.1 %copy-start = (bf16[1024,1024,1]{1,0,2:T(8,128)(2,1)S(1)}, bf16[1024,1024,1]{1,0,2:T(8,128)(2,1)}, u32[]{:S(2)}) copy-start(bf16[1024,1024,1]{1,0,2:T(8,128)(2,1)} %reshape.77) | copy-start | bytes 6291460
Sparse Core Ops, SparseCore 0:
  47.2 37.9 all-gather.3

commit v2 on v1

v2 whole, which is shorter than its diff:
```python
import jax
import jax.numpy as jnp
from jax import lax
from jax.experimental import pallas as pl
from jax.experimental.pallas import tpu as pltpu
from jax.sharding import Mesh
from jax.sharding import PartitionSpec as P

ROW = ("z", "core")
COL = ("x", "y")
ALL = ROW + COL


def size_of(axes):
    axes = axes if isinstance(axes, tuple) else (axes,)
    count = 1
    for axis in axes:
        count *= lax.axis_size(axis)
    return count


def sent_to_all(value, axes):
    copies = jnp.broadcast_to(value, (size_of(axes), *value.shape))
    return lax.all_to_all(copies, axes, split_axis=0, concat_axis=0, tiled=True)


def column_tiles(panel, col, rows, cols):
    odd = lax.rem(col, 2)
    pair = panel.shape[0] // 2

    def moved(flip):
        half = lax.bitwise_xor(odd, flip)
        part = lax.dynamic_slice_in_dim(panel, pair * half, pair, 0)
        pairs = [
            (r * cols + c, (c // 2) * cols + 2 * r + ((c % 2) ^ flip))
            for r in range(rows)
            for c in range(cols)
        ]
        return lax.ppermute(part, ALL, pairs)

    first, second = moved(0), moved(1)
    low = jnp.where(odd == 0, first, second)
    high = jnp.where(odd == 0, second, first)
    return jnp.concatenate([low, high], axis=1)


LANES = 128
STEP = 2 * LANES


def solve_and_pair(ranks, packed, full, shares, core_blocks, values, factor, solved):
    cols, tiles, depth, width = full.shape
    rows = packed.shape[0]
    pair = core_blocks.shape[1]
    half = depth // 2
    steps = cols * depth // STEP
    group = cols // steps
    count = cols * half
    row = lax.axis_index(ROW)
    col = lax.axis_index(COL)
    lane = lax.broadcasted_iota(jnp.int32, (1, 1, width), 2)

    for z in range(rows // 2):
        for k in range(2):
            for g in range(steps):
                factor[pl.ds(LANES * z, LANES), pl.ds(STEP * g + LANES * k, LANES)] = packed[
                    2 * z + k, pl.ds(LANES * g, LANES), :
                ]

    def fill_own(t, carry):
        keep = (lane < ranks[row * tiles + t]).astype(jnp.bfloat16)
        for k in range(2):
            part = full[:, t, pl.ds(half * k, half), :] * keep
            for g in range(steps):
                values[t, pl.ds(STEP * g + LANES * k, LANES), :] = part[
                    group * g : group * (g + 1)
                ].reshape(LANES, width)
        return carry

    lax.fori_loop(0, tiles, fill_own, 0)

    part_rows = 2 * depth
    for u in range(pair):
        for h in range(width // LANES):
            keep = (lane[:, :, LANES * h : LANES * (h + 1)] < ranks[col * pair + u]).astype(
                jnp.bfloat16
            )
            start = count + (h * pair + u) * part_rows
            part = (packed[:, pl.ds(start, part_rows), :] * keep).reshape(cols, depth, LANES)
            for k in range(2):
                piece = part[:, half * k : half * (k + 1), :]
                for g in range(steps):
                    values[
                        tiles + u,
                        pl.ds(STEP * g + LANES * k, LANES),
                        pl.ds(LANES * h, LANES),
                    ] = piece[group * g : group * (g + 1)].reshape(LANES, LANES)

    def solve(t, carry):
        for i in range(steps):
            known = STEP * (i + 1)
            block = pl.ds(STEP * i, STEP)
            solved[t, block, :] = jnp.dot(
                factor[block, :known], values[t, :known, :], preferred_element_type=jnp.float32
            ).astype(jnp.bfloat16)
        return carry

    lax.fori_loop(0, tiles + pair, solve, 0)
    first = pl.multiple_of(col * depth, depth)
    for t in range(tiles):
        shares[t] = solved[t, pl.ds(first, depth), :]

    def blocks(t, carry):
        for u in range(pair):
            core_blocks[t, u] = lax.dot_general(
                solved[t],
                solved[tiles + u],
                (((0,), (0,)), ((), ())),
                preferred_element_type=jnp.float32,
            ).astype(jnp.bfloat16)
        return carry

    lax.fori_loop(0, tiles, blocks, 0)


def finish(ranks, packed, full, pair):
    cols, tiles, depth, width = full.shape
    in_vmem = pl.BlockSpec(memory_space=pltpu.VMEM)
    height = cols * depth
    return pl.pallas_call(
        solve_and_pair,
        out_shape=(
            jax.ShapeDtypeStruct((tiles, depth, width), jnp.bfloat16),
            jax.ShapeDtypeStruct((tiles, pair, width, width), jnp.bfloat16),
        ),
        in_specs=[pl.BlockSpec(memory_space=pltpu.SMEM), in_vmem, in_vmem],
        out_specs=(in_vmem, in_vmem),
        scratch_shapes=[
            pltpu.VMEM((tiles + pair, height, width), jnp.bfloat16),
            pltpu.VMEM((height, height), jnp.bfloat16),
            pltpu.VMEM((tiles + pair, height, width), jnp.bfloat16),
        ],
        compiler_params=pltpu.CompilerParams(vmem_limit_bytes=40 << 20),
        cost_estimate=pl.CostEstimate(
            flops=2 * height * height * width * (tiles + pair), bytes_accessed=8 << 20, transcendentals=0
        ),
    )(ranks, packed, full)


def per_device(panel, inverse_factor, ranks):
    tiles, depth, width = panel.shape
    core = lax.axis_index("core")
    col = lax.axis_index(COL)
    rows, cols = size_of(ROW), size_of(COL)
    pair = tiles * rows // cols

    part = column_tiles(panel, col, rows, cols)

    factor = lax.all_gather(inverse_factor.T, "core", axis=1, tiled=True)
    half = depth // 2
    factor = lax.dynamic_slice_in_dim(factor, half * core, half, 0)
    factor = sent_to_all(factor, COL).reshape(-1, LANES, LANES)
    factor = factor.transpose(0, 2, 1).reshape(-1, LANES)

    sides = width // LANES
    side_parts = [part[:, :, LANES * h : LANES * (h + 1)].reshape(-1, LANES) for h in range(sides)]
    packed = lax.all_gather(jnp.concatenate([factor, *side_parts], axis=0), ROW)

    full = sent_to_all(sent_to_all(panel, "y"), "x").reshape(cols, tiles, depth, width)
    return finish(ranks, packed, full, pair)


def solution(mesh):
    split = Mesh(mesh.devices.reshape(8, 2, 4, 8), ALL)
    return jax.shard_map(
        per_device,
        mesh=split,
        in_specs=(P(ROW, COL, None), P(ROW, COL), P()),
        out_specs=(P(ROW, COL, None), P(ROW, COL, None, None)),
        check_vma=False,
    )
```

time: 130 us -> 111 us (0.85)
  blocking collectives: 22.4 us -> 49.3 us
  waiting for transfers between devices: 34.4 us -> 10.5 us
  local copies, waits for them, and re-layouts: 16.9 us -> 4.74 us
  matrix products: 10.4 us -> 0 us
  Pallas kernels: 0 us -> 7.23 us
  starting transfers between devices: 27.7 us -> 24 us
  other arithmetic: 3.59 us -> 0.72 us
    all_to_all x1 -> x2, blocking collectives: 19.4 us -> 46.3 us  [sent_to_all(): return lax.all_to_all(copies, axes, split_axis=0, concat_axis=0, tiled=True)]
    all_to_all x2 -> x1, waiting for transfers between devices: 34.4 us -> 10.5 us  [sent_to_all(): return lax.all_to_all(copies, axes, split_axis=0, concat_axis=0, tiled=True)]
    dot_general x2 -> x0, matrix products: 10.4 us -> none  [the longest x1 6.11 us: solve(): jnp.einsum('ba,tbr->tar', whole, value, preferred_element_type=jnp.float32)]
    pallas_call x0 -> x1, Pallas kernels: none -> 7.23 us  [finish(): pl.pallas_call(solve_and_pair, out_shape=(jax.ShapeDtypeStruct((tiles, de...]
    all_to_all x2 -> x1, starting transfers between devices: 19 us -> 15.3 us  [sent_to_all(): return lax.all_to_all(copies, axes, split_axis=0, concat_axis=0, tiled=True)]
    slice x2 -> x0, local copies, waits for them, and re-layouts: 3.05 us -> none  [the longest x1 1.75 us: per_device(): whole = packed[:, :count].reshape(rows // 2, 2, cols, half, lanes)]
    mul x2 -> x0, other arithmetic: 2.74 us -> none  [kept(): value * (columns[None, :] < ranks[:, None]).astype(value.dtype)[:, None, :]]
    reshape x2 -> x0, local copies, waits for them, and re-layouts: 2.34 us -> none  [the longest x1 2.31 us: per_device(): whole = whole.transpose(2, 1, 3, 0, 4).reshape(cols * depth, -1)]
  transfers between devices with their start and end apart: 5 -> 4, of which waited for: 2 -> 1; matrix products, arithmetic and copies ran while one was open for 4% -> 2% of each run, Pallas kernels for 0% -> 0%
where the time goes in v2:
time: 111 us
  blocking collectives  49.3 us (44%)
  starting transfers between devices  24 us (22%)
  between operations  14.1 us (13%)
  waiting for transfers between devices  10.5 us (9%)
  Pallas kernels  7.23 us (7%)
  local copies, waits for them, and re-layouts  4.74 us (4%)
    all_to_all x2, blocking collectives, sent_to_all(): return lax.all_to_all(copies, axes, split_axis=0, concat_axis=0, tiled=True)  46.3 us
    all_to_all x1, starting transfers between devices, sent_to_all(): return lax.all_to_all(copies, axes, split_axis=0, concat_axis=0, tiled=True)  15.3 us
    all_to_all x1, waiting for transfers between devices, sent_to_all(): return lax.all_to_all(copies, axes, split_axis=0, concat_axis=0, tiled=True)  10.5 us
    ppermute x2, starting transfers between devices, moved(): return lax.ppermute(part, ALL, pairs)  8.64 us
    pallas_call x1, Pallas kernels, finish(): pl.pallas_call(solve_and_pair, out_shape=(jax.ShapeDtypeStruct((tiles, de...  7.23 us
    all_gather x1, blocking collectives, per_device(): factor = lax.all_gather(inverse_factor.T, 'core', axis=1, tiled=True)  3.04 us
  transfers between devices with their start and end apart: 4, of which 1 were waited for; matrix products, arithmetic and copies ran while one was open for 2% of the time, Pallas kernels for 0%

profile of v2, /device:TPU:128, one launch (start us, length us, event | category | flops | bytes accessed | tf_op | source)
XLA Modules:
  0.0 110.7 jit_solution(14712918413061562152)
XLA Ops:
  7.2 0.8 constant_dynamic-slice_fusion.1
  8.0 1.9 %collective-permute-start = (bf16[2,32,256]{2,1,0:T(8,128)(2,1)S(1)}, bf16[2,32,256]{2,1,0:T(8,128)(2,1)S(1)}, u32[]{:S(2)}, u32[]{:S(2)}) collective-permute-start(bf16[2,32,256]{2,1,0:T(8,128)(2,1)S(1)} %get-tuple-element.6), channel_id=1, source_target_pairs={{0,0},{1,1},{2,32},{3,33},{4,64},{5,65},{6,96},{7,97},{8,128},{9,1... | collective-permute-start | bytes 98312 | tf_op jit(solution)/shard_map/ppermute | solution.py:39
  9.9 6.7 %collective-permute-start.1 = (bf16[2,32,256]{2,1,0:T(8,128)(2,1)S(1)}, bf16[2,32,256]{2,1,0:T(8,128)(2,1)S(1)}, u32[]{:S(2)}, u32[]{:S(2)}) collective-permute-start(bf16[2,32,256]{2,1,0:T(8,128)(2,1)S(1)} %get-tuple-element.7), channel_id=1, source_target_pairs={{0,1},{1,0},{2,33},{3,32},{4,65},{5,64},{6,97},{7,96},{8,129},{9,1... | collective-permute-start | bytes 98312 | tf_op jit(solution)/shard_map/ppermute | solution.py:39
  16.6 3.0 %all-gather.1 = bf16[2,64,32]{1,2,0:T(8,128)(2,1)S(1)} all-gather(bf16[1,64,32]{1,2,0:T(8,128)(2,1)} %bitcast.19), channel_id=1, replica_groups=mesh['z'=8,'core'=2,'x'=4,'y'=8] {'core'}, dimensions={0}, use_global_device_ids=true | all-gather | bytes 12288 | tf_op jit(solution)/shard_map/all_gather | solution.py:159
  19.7 0.1 reshape.26
  19.8 0.7 broadcast_in_dim.9
  20.5 15.3 %all-to-all-start = ((bf16[32,16,128]{2,1,0:T(8,128)(2,1)}), bf16[32,16,128]{2,1,0:T(8,128)(2,1)S(1)}, u32[]{:S(2)}, u32[]{:S(2)}) async-start(bf16[32,16,128]{2,1,0:T(8,128)(2,1)} %broadcast_in_dim.9), calls=%async_computation | async-start | bytes 262144 | tf_op jit(solution)/shard_map/all_to_all | solution.py:24
  35.8 0.0 all-gather.4.cloned.1.call-start
  35.8 0.0 collective-permute-done
  35.8 0.0 collective-permute-done.1
  35.9 10.5 %all-to-all-done = bf16[32,16,128]{2,1,0:T(8,128)(2,1)S(1)} async-done(((bf16[32,16,128]{2,1,0:T(8,128)(2,1)}), bf16[32,16,128]{2,1,0:T(8,128)(2,1)S(1)}, u32[]{:S(2)}, u32[]{:S(2)}) %all-to-all-start) | async-done | bytes 131104 | tf_op jit(solution)/shard_map/all_to_all | solution.py:24
  46.4 0.1 copy.10
  46.5 0.7 pad_maximum_fusion
  47.2 0.0 all-gather.4.cloned.1.call-update
  47.3 0.9 broadcast_in_dim.10
  48.2 19.4 %all_to_all.15 = bf16[8,4,32,256]{3,2,1,0:T(8,128)(2,1)S(1)} all-to-all(bf16[8,4,32,256]{3,2,1,0:T(8,128)(2,1)S(1)} %broadcast_in_dim.10), channel_id=1, replica_groups=mesh['z'=8,'core'=2,'x'=4,'y'=8] {'y'}, dimensions={0} | all-to-all | bytes 1048576 | tf_op jit(solution)/shard_map/all_to_all | solution.py:24
  67.5 0.3 broadcast_in_dim.11
  67.8 0.0 copy-start.1
  67.8 26.9 %all_to_all.16 = bf16[4,8,4,32,256]{4,3,2,1,0:T(8,128)(2,1)S(1)} all-to-all(bf16[4,8,4,32,256]{4,3,2,1,0:T(8,128)(2,1)S(1)} %broadcast_in_dim.11), channel_id=1, replica_groups=mesh['z'=8,'core'=2,'x'=4,'y'=8] {'x'}, dimensions={0} | all-to-all | bytes 4194304 | tf_op jit(solution)/shard_map/all_to_all | solution.py:24
  94.7 0.0 all-gather.4.cloned.1.call-done
  94.7 0.0 copy-done.1
  94.7 0.0 copy-start
  94.7 1.9 %copy-done = bf16[12288,128]{1,0:T(8,128)(2,1)S(1)} copy-done((bf16[12288,128]{1,0:T(8,128)(2,1)S(1)}, bf16[12288,128]{1,0:T(8,128)(2,1)}, u32[]{:S(2)}) %copy-start) | copy-done | bytes 3145752
  96.6 7.2 %shard_map.50 = (bf16[4,32,256]{2,1,0:T(8,128)(2,1)}, bf16[4,2,256,256]{3,2,1,0:T(8,128)(2,1)}) custom-call(s32[64]{0:T(128)S(1)} %copy-done.1, bf16[16,768,128]{2,1,0:T(8,128)(2,1)S(1)} %bitcast.14, bf16[32,4,32,256]{3,2,1,0:T(8,128)(2,1)S(1)} %bitcast.13), custom_call_target="tpu_custom_call" | custom-call | flops 3221225472 | bytes 8388608 | tf_op jit(solution)/shard_map/pallas_call | solution.py:130
  (4 shorter events, 0.0 us)
Async XLA Ops:
  8.0 27.9 %collective-permute-start = (bf16[2,32,256]{2,1,0:T(8,128)(2,1)S(1)}, bf16[2,32,256]{2,1,0:T(8,128)(2,1)S(1)}, u32[]{:S(2)}, u32[]{:S(2)}) collective-permute-start(bf16[2,32,256]{2,1,0:T(8,128)(2,1)S(1)} %get-tuple-element.6), channel_id=1, source_target_pairs={{0,0},{1,1},{2,32},{3,33},{4,64},{5,65},{6,96},{7,97},{8,128},{9,1... | collective-permute-start | bytes 98312 | tf_op jit(solution)/shard_map/ppermute | solution.py:39
  9.9 25.9 %collective-permute-start.1 = (bf16[2,32,256]{2,1,0:T(8,128)(2,1)S(1)}, bf16[2,32,256]{2,1,0:T(8,128)(2,1)S(1)}, u32[]{:S(2)}, u32[]{:S(2)}) collective-permute-start(bf16[2,32,256]{2,1,0:T(8,128)(2,1)S(1)} %get-tuple-element.7), channel_id=1, source_target_pairs={{0,1},{1,0},{2,33},{3,32},{4,65},{5,64},{6,97},{7,96},{8,129},{9,1... | collective-permute-start | bytes 98312 | tf_op jit(solution)/shard_map/ppermute | solution.py:39
  20.5 25.9 %all-to-all-start = ((bf16[32,16,128]{2,1,0:T(8,128)(2,1)}), bf16[32,16,128]{2,1,0:T(8,128)(2,1)S(1)}, u32[]{:S(2)}, u32[]{:S(2)}) async-start(bf16[32,16,128]{2,1,0:T(8,128)(2,1)} %broadcast_in_dim.9), calls=%async_computation | async-start | bytes 262144 | tf_op jit(solution)/shard_map/all_to_all | solution.py:24
  35.8 59.0 %all-gather.4.cloned.1.call-start = ((), (), s32[]{:S(2)}) async-start(), calls=%async_computation.3 | async-start | bytes 3342336 | tf_op jit(solution)/shard_map/all_gather | solution.py:167
  67.8 26.9 %copy-start.1 = (s32[64]{0:T(128)S(1)}, s32[64]{0:T(128)}, u32[]{:S(2)}) copy-start(s32[64]{0:T(128)} %ranks.1) | copy-start | bytes 772
  94.7 1.9 %copy-start = (bf16[12288,128]{1,0:T(8,128)(2,1)S(1)}, bf16[12288,128]{1,0:T(8,128)(2,1)}, u32[]{:S(2)}) copy-start(bf16[12288,128]{1,0:T(8,128)(2,1)} %all-gather.4.cloned.1.call-done) | copy-start | bytes 9437188
Sparse Core Ops, SparseCore 0:
  47.4 37.9 all-gather.3

commit v3 on v1

v3 whole, which is shorter than its diff:
```python
import jax
import jax.numpy as jnp
from jax import lax
from jax.experimental import pallas as pl
from jax.experimental.pallas import tpu as pltpu
from jax.sharding import Mesh
from jax.sharding import PartitionSpec as P


ROW = ("z", "core")
COL = ("x", "y")
ALL = ROW + COL


def size_of(axes):
    axes = axes if isinstance(axes, tuple) else (axes,)
    count = 1
    for axis in axes:
        count *= lax.axis_size(axis)
    return count


def copies_for(value, axes):
    return jnp.broadcast_to(value, (size_of(axes), *value.shape))


def exchanged(copies, axes):
    return lax.all_to_all(copies, axes, split_axis=0, concat_axis=0, tiled=True)


def column_tiles(panel, col, rows, cols):
    odd = lax.rem(col, 2)
    pair = panel.shape[0] // 2

    def moved(flip):
        half = lax.bitwise_xor(odd, flip)
        part = lax.dynamic_slice_in_dim(panel, pair * half, pair, 0)
        pairs = [
            (r * cols + c, (c // 2) * cols + 2 * r + ((c % 2) ^ flip))
            for r in range(rows)
            for c in range(cols)
        ]
        return lax.ppermute(part, ALL, pairs)

    first, second = moved(0), moved(1)
    low = jnp.where(odd == 0, first, second)
    high = jnp.where(odd == 0, second, first)
    return jnp.concatenate([low, high], axis=1)


NEAR = (0, 2, 6, 4)
ODD = (1, 3, 7, 5)
STEP = 256
IN_VMEM = pl.BlockSpec(memory_space=pltpu.VMEM)
IN_SMEM = pl.BlockSpec(memory_space=pltpu.SMEM)


def columns_kept(rank, width):
    lane = lax.broadcasted_iota(jnp.int32, (1, width), 1)
    return (lane < rank).astype(jnp.bfloat16)


def solve_block(factor, known_rows, keep, i):
    block = jnp.dot(
        factor[pl.ds(STEP * i, STEP), : STEP * (i + 1)],
        known_rows,
        preferred_element_type=jnp.float32,
    )
    return block.astype(jnp.bfloat16) * keep


def column_kernel(ranks, here, there, factor, solved, values):
    order = factor.shape[1]
    pair, _, width = solved.shape
    height = here.shape[1]
    col = lax.axis_index(COL)
    level = lax.axis_index("z")
    core = lax.axis_index("core")
    levels = lax.axis_size("z")
    for source, k in ((here, core), (there, 1 - core)):
        for n, shift in enumerate(NEAR + ODD):
            row = 2 * lax.rem(level + shift, levels) + k
            place = pl.ds(pl.multiple_of(height * row, height), height)
            factor[place, :] = source[n, :, :order]
            for u in range(pair):
                values[u, place, :] = source[n, :, order + width * u : order + width * (u + 1)]

    for u in range(pair):
        keep = columns_kept(ranks[col * pair + u], width)
        for i in range(order // STEP):
            solved[u, pl.ds(STEP * i, STEP), :] = solve_block(
                factor, values[u, : STEP * (i + 1), :], keep, i
            )


def solve_columns(ranks, here, there, pair, width, order):
    return pl.pallas_call(
        column_kernel,
        out_shape=(
            jax.ShapeDtypeStruct((order, order), jnp.bfloat16),
            jax.ShapeDtypeStruct((pair, order, width), jnp.bfloat16),
        ),
        in_specs=[IN_SMEM, IN_VMEM, IN_VMEM],
        out_specs=(IN_VMEM, IN_VMEM),
        scratch_shapes=[pltpu.VMEM((pair, order, width), jnp.bfloat16)],
        compiler_params=pltpu.CompilerParams(vmem_limit_bytes=16 << 20),
        cost_estimate=pl.CostEstimate(
            flops=2 * order * order * width * pair, bytes_accessed=6 << 20, transcendentals=0
        ),
    )(ranks, here, there)


def row_kernel(ranks, factor_in, others_in, full, shares, core_blocks, factor, others, solved, sems):
    _, tiles, depth, width = full.shape
    pair, order, _ = others.shape
    row = lax.axis_index(ROW)
    col = lax.axis_index(COL)
    steps = order // STEP

    def brought(i):
        if i == steps:
            return pltpu.make_async_copy(others_in, others, sems.at[i])
        block = pl.ds(STEP * i, STEP)
        return pltpu.make_async_copy(factor_in.at[block, :], factor.at[block, :], sems.at[i])

    for i in range(steps + 1):
        brought(i).start()

    def one(t, carry):
        keep = columns_kept(ranks[row * tiles + t], width)
        for i in range(steps):

            @pl.when(t == 0)
            def _():
                brought(i).wait()

            known = full[: STEP * (i + 1) // depth, t].reshape(STEP * (i + 1), width)
            solved[pl.ds(STEP * i, STEP), :] = solve_block(factor, known, keep, i)
        shares[t] = solved[pl.ds(pl.multiple_of(col * depth, depth), depth), :]

        @pl.when(t == 0)
        def _():
            brought(steps).wait()

        for u in range(pair):
            core_blocks[t, u] = lax.dot_general(
                solved[...],
                others[u],
                (((0,), (0,)), ((), ())),
                preferred_element_type=jnp.float32,
            ).astype(jnp.bfloat16)
        return carry

    lax.fori_loop(0, tiles, one, 0)


def solve_rows(ranks, factor, others, full):
    _, tiles, depth, width = full.shape
    pair, order, _ = others.shape
    in_hbm = pl.BlockSpec(memory_space=pltpu.HBM)
    return pl.pallas_call(
        row_kernel,
        out_shape=(
            jax.ShapeDtypeStruct((tiles, depth, width), jnp.bfloat16),
            jax.ShapeDtypeStruct((tiles, pair, width, width), jnp.bfloat16),
        ),
        in_specs=[IN_SMEM, in_hbm, in_hbm, IN_VMEM],
        out_specs=(IN_VMEM, IN_VMEM),
        scratch_shapes=[
            pltpu.VMEM((order, order), jnp.bfloat16),
            pltpu.VMEM((pair, order, width), jnp.bfloat16),
            pltpu.VMEM((order, width), jnp.bfloat16),
            pltpu.SemaphoreType.DMA((order // STEP + 1,)),
        ],
        compiler_params=pltpu.CompilerParams(vmem_limit_bytes=24 << 20),
        cost_estimate=pl.CostEstimate(
            flops=3 * order * order * width * tiles, bytes_accessed=6 << 20, transcendentals=0
        ),
    )(ranks, factor, others, full)


def from_level(value, shift):
    levels = lax.axis_size("z")
    return lax.ppermute(value, "z", [((z + shift) % levels, z) for z in range(levels)])


def per_device(panel, inverse_factor, ranks):
    tiles, depth, width = panel.shape
    col = lax.axis_index(COL)
    rows, cols = size_of(ROW), size_of(COL)
    pair = tiles * rows // cols
    order = cols * depth

    part = column_tiles(panel, col, rows, cols)
    factor = exchanged(copies_for(inverse_factor.T, COL), COL).reshape(order, -1).T

    packed = jnp.concatenate([factor, *part], axis=1)[None]
    copies, packed = lax.optimization_barrier((copies_for(panel, "y"), packed))
    along_y = exchanged(copies, "y")
    opposite, above, below = from_level(packed, 4), from_level(packed, 2), from_level(packed, 6)
    copies, opposite, above, below = lax.optimization_barrier(
        (copies_for(along_y, "x"), opposite, above, below)
    )
    full = exchanged(copies, "x")
    full = full.reshape(cols, tiles, depth, width)
    upper, lower = jnp.concatenate([packed, above]), jnp.concatenate([packed, below])
    upper = from_level(upper, 1)
    lower = from_level(lower, 7)
    here = jnp.concatenate([packed, above, below, opposite, upper, lower])
    there = lax.ppermute(here, "core", [(0, 1), (1, 0)])
    factor, others = solve_columns(ranks, here, there, pair, width, order)
    return solve_rows(ranks, factor, others, full)


def solution(mesh):
    split = Mesh(mesh.devices.reshape(8, 2, 4, 8), ALL)
    return jax.shard_map(
        per_device,
        mesh=split,
        in_specs=(P(ROW, COL, None), P(ROW, COL), P()),
        out_specs=(P(ROW, COL, None), P(ROW, COL, None, None)),
        check_vma=False,
    )
```

time: 130 us -> 135 us (1.038)
  the two profiles are of different devices: /device:TPU:128 before, /device:TPU:1 now
where the time goes in v3:
time: 135 us
  starting transfers between devices  62.1 us (46%)
  waiting for transfers between devices  47.6 us (35%)
  local copies, waits for them, and re-layouts  12.4 us (9%)
  Pallas kernels  11.7 us (9%)
    all_to_all x3, waiting for transfers between devices, exchanged(): return lax.all_to_all(copies, axes, split_axis=0, concat_axis=0, tiled=True)  31.2 us
    ppermute x5, starting transfers between devices, from_level(): lax.ppermute(value, 'z', [((z + shift) % levels, z) for z in range(levels)])  26.4 us
    all_to_all x3, starting transfers between devices, exchanged(): return lax.all_to_all(copies, axes, split_axis=0, concat_axis=0, tiled=True)  23.1 us
    ppermute x5, waiting for transfers between devices, from_level(): lax.ppermute(value, 'z', [((z + shift) % levels, z) for z in range(levels)])  16.4 us
    pallas_call x1, Pallas kernels, solve_rows(): pl.pallas_call(row_kernel, out_shape=(jax.ShapeDtypeStruct((tiles, depth,...  8.72 us
    ppermute x2, starting transfers between devices, moved(): return lax.ppermute(part, ALL, pairs)  8.52 us
    unnamed x15, local copies, waits for them, and re-layouts  7.51 us
    ppermute x1, starting transfers between devices, per_device(): there = lax.ppermute(here, 'core', [(0, 1), (1, 0)])  4.1 us
  transfers between devices with their start and end apart: 11, of which 4 were waited for; matrix products, arithmetic and copies ran while one was open for 4% of the time, Pallas kernels for 2%

profile of v3, /device:TPU:1, one launch (start us, length us, event | category | flops | bytes accessed | tf_op | source)
XLA Modules:
  0.0 134.7 jit_solution(14541515110997887413)
XLA Ops:
  0.7 0.8 constant_dynamic-slice_fusion.1
  1.5 5.6 %collective-permute-start = (bf16[2,32,256]{2,1,0:T(8,128)(2,1)S(1)}, bf16[2,32,256]{2,1,0:T(8,128)(2,1)S(1)}, u32[]{:S(2)}, u32[]{:S(2)}) collective-permute-start(bf16[2,32,256]{2,1,0:T(8,128)(2,1)S(1)} %get-tuple-element.24), channel_id=1, source_target_pairs={{0,0},{1,1},{2,32},{3,33},{4,64},{5,65},{6,96},{7,97},{8,128},{9,1... | collective-permute-start | bytes 98312 | tf_op jit(solution)/shard_map/ppermute | solution.py:43
  7.1 2.9 %collective-permute-start.1 = (bf16[2,32,256]{2,1,0:T(8,128)(2,1)S(1)}, bf16[2,32,256]{2,1,0:T(8,128)(2,1)S(1)}, u32[]{:S(2)}, u32[]{:S(2)}) collective-permute-start(bf16[2,32,256]{2,1,0:T(8,128)(2,1)S(1)} %get-tuple-element.25), channel_id=1, source_target_pairs={{0,1},{1,0},{2,33},{3,32},{4,65},{5,64},{6,97},{7,96},{8,129},{9,1... | collective-permute-start | bytes 98312 | tf_op jit(solution)/shard_map/ppermute | solution.py:43
  10.0 0.7 broadcast_in_dim.13
  10.7 0.8 reshape.12
  11.6 15.9 %all-to-all-start = ((bf16[32,2,1024]{2,1,0:T(2,128)(2,1)}), bf16[32,2,1024]{2,1,0:T(2,128)(2,1)S(1)}, u32[]{:S(2)}, u32[]{:S(2)}) async-start(bf16[32,2,1024]{2,1,0:T(2,128)(2,1)} %reshape.12), calls=%async_computation | async-start | bytes 262144 | tf_op jit(solution)/shard_map/all_to_all | solution.py:28
  27.6 9.1 %all-to-all-done = bf16[32,2,1024]{2,1,0:T(2,128)(2,1)S(1)} async-done(((bf16[32,2,1024]{2,1,0:T(2,128)(2,1)}), bf16[32,2,1024]{2,1,0:T(2,128)(2,1)S(1)}, u32[]{:S(2)}, u32[]{:S(2)}) %all-to-all-start) | async-done | bytes 131104 | tf_op jit(solution)/shard_map/all_to_all | solution.py:28
  36.7 0.2 reshape.13
  36.9 0.1 copy.6
  37.1 0.9 broadcast_in_dim.12
  38.0 3.5 %all-to-all-start.1 = ((bf16[8,4,32,256]{3,2,1,0:T(8,128)(2,1)}), bf16[8,4,32,256]{3,2,1,0:T(8,128)(2,1)S(1)}, u32[]{:S(2)}, u32[]{:S(2)}) async-start(bf16[8,4,32,256]{3,2,1,0:T(8,128)(2,1)} %broadcast_in_dim.12), calls=%async_computation.1 | async-start | bytes 1048576 | tf_op jit(solution)/shard_map/all_to_all | solution.py:28
  41.5 5.5 %collective-permute-start.4 = (bf16[1,64,1536]{2,1,0:T(8,128)(2,1)S(1)}, bf16[1,64,1536]{2,1,0:T(8,128)(2,1)S(1)}, u32[]{:S(2)}, u32[]{:S(2)}) collective-permute-start(bf16[1,64,1536]{2,1,0:T(8,128)(2,1)S(1)} %maximum_bitcast_fusion), channel_id=1, source_target_pairs={{384,0},{448,64},{0,128},{64,192},{128,256},{192,320},{256,384},{3... | collective-permute-start | bytes 589832 | tf_op jit(solution)/shard_map/ppermute | solution.py:184
  47.0 5.5 %collective-permute-start.3 = (bf16[1,64,1536]{2,1,0:T(8,128)(2,1)S(1)}, bf16[1,64,1536]{2,1,0:T(8,128)(2,1)S(1)}, u32[]{:S(2)}, u32[]{:S(2)}) collective-permute-start(bf16[1,64,1536]{2,1,0:T(8,128)(2,1)S(1)} %maximum_bitcast_fusion), channel_id=1, source_target_pairs={{128,0},{192,64},{256,128},{320,192},{384,256},{448,320},{0,384},{... | collective-permute-start | bytes 589832 | tf_op jit(solution)/shard_map/ppermute | solution.py:184
  52.5 4.5 %collective-permute-start.2 = (bf16[1,64,1536]{2,1,0:T(8,128)(2,1)S(1)}, bf16[1,64,1536]{2,1,0:T(8,128)(2,1)S(1)}, u32[]{:S(2)}, u32[]{:S(2)}) collective-permute-start(bf16[1,64,1536]{2,1,0:T(8,128)(2,1)S(1)} %maximum_bitcast_fusion), channel_id=1, source_target_pairs={{256,0},{320,64},{384,128},{448,192},{0,256},{64,320},{128,384},{1... | collective-permute-start | bytes 589832 | tf_op jit(solution)/shard_map/ppermute | solution.py:184
  57.0 0.7 constant_dynamic-update-slice_fusion.5
  57.7 9.0 %collective-permute-done.2 = bf16[1,64,1536]{2,1,0:T(8,128)(2,1)S(1)} collective-permute-done((bf16[1,64,1536]{2,1,0:T(8,128)(2,1)S(1)}, bf16[1,64,1536]{2,1,0:T(8,128)(2,1)S(1)}, u32[]{:S(2)}, u32[]{:S(2)}) %collective-permute-start.2) | collective-permute-done | bytes 196640 | tf_op jit(solution)/shard_map/ppermute | solution.py:184
  66.8 1.6 %broadcast_in_dim.15 = bf16[4,8,4,32,256]{4,3,2,1,0:T(8,128)(2,1)} broadcast(bf16[8,4,32,256]{3,2,1,0:T(8,128)(2,1)S(1)} %all-to-all-done.1), dimensions={1,2,3,4} | broadcast | bytes 2621440 | tf_op jit(solution)/shard_map/broadcast_in_dim | solution.py:24
  68.4 9.0 %collective-permute-start.6 = (bf16[2,64,1536]{2,1,0:T(8,128)(2,1)S(1)}, bf16[2,64,1536]{2,1,0:T(8,128)(2,1)S(1)}, u32[]{:S(2)}, u32[]{:S(2)}) collective-permute-start(bf16[2,64,1536]{2,1,0:T(8,128)(2,1)S(1)} %get-tuple-element.18), channel_id=1, source_target_pairs={{448,0},{0,64},{64,128},{128,192},{192,256},{256,320},{320,384},{3... | collective-permute-start | bytes 1179656 | tf_op jit(solution)/shard_map/ppermute | solution.py:184
  77.4 1.9 %collective-permute-start.5 = (bf16[2,64,1536]{2,1,0:T(8,128)(2,1)S(1)}, bf16[2,64,1536]{2,1,0:T(8,128)(2,1)S(1)}, u32[]{:S(2)}, u32[]{:S(2)}) collective-permute-start(bf16[2,64,1536]{2,1,0:T(8,128)(2,1)S(1)} %get-tuple-element.19), channel_id=1, source_target_pairs={{64,0},{128,64},{192,128},{256,192},{320,256},{384,320},{448,384},... | collective-permute-start | bytes 1179656 | tf_op jit(solution)/shard_map/ppermute | solution.py:184
  79.3 0.7 constant_dynamic-update-slice_fusion.4
  80.0 0.7 constant_dynamic-update-slice_fusion.3
  80.7 0.7 constant_dynamic-update-slice_fusion.2
  81.4 7.3 %collective-permute-done.5 = bf16[2,64,1536]{2,1,0:T(8,128)(2,1)S(1)} collective-permute-done((bf16[2,64,1536]{2,1,0:T(8,128)(2,1)S(1)}, bf16[2,64,1536]{2,1,0:T(8,128)(2,1)S(1)}, u32[]{:S(2)}, u32[]{:S(2)}) %collective-permute-start.5) | collective-permute-done | bytes 393248 | tf_op jit(solution)/shard_map/ppermute | solution.py:184
  88.8 0.8 constant_dynamic-update-slice_fusion.1
  89.5 0.8 constant_dynamic-update-slice_fusion.here
  90.3 4.1 %collective-permute-start.7 = (bf16[8,64,1536]{2,1,0:T(8,128)(2,1)}, bf16[8,64,1536]{2,1,0:T(8,128)(2,1)}, u32[]{:S(2)}, u32[]{:S(2)}) collective-permute-start(bf16[8,64,1536]{2,1,0:T(8,128)(2,1)} %constant_dynamic-update-slice_fusion.here), channel_id=1, source_target_pairs={{0,32},{32,0},{1,33},{33,1},{2,34},{34,2},{3,35},{35,3},{4,36},{36... | collective-permute-start | bytes 4718600 | tf_op jit(solution)/shard_map/ppermute | solution.py:210
  94.4 3.6 %all-to-all-start.2 = ((bf16[4,8,4,32,256]{4,3,2,1,0:T(8,128)(2,1)}), bf16[4,8,4,32,256]{4,3,2,1,0:T(8,128)(2,1)S(1)}, u32[]{:S(2)}, u32[]{:S(2)}) async-start(bf16[4,8,4,32,256]{4,3,2,1,0:T(8,128)(2,1)} %broadcast_in_dim.15), calls=%async_computation.2 | async-start | bytes 4194304 | tf_op jit(solution)/shard_map/all_to_all | solution.py:28
  98.1 2.9 %shard_map.50 = (bf16[1024,1024]{1,0:T(8,128)(2,1)S(1)}, bf16[2,1024,256]{2,1,0:T(8,128)(2,1)S(1)}) custom-call(s32[64]{0:T(128)S(1)} %copy-done, bf16[8,64,1536]{2,1,0:T(8,128)(2,1)} %constant_dynamic-update-slice_fusion.here, bf16[8,64,1536]{2,1,0:T(8,128)(2,1)} %collective-permute-done.7.there), custom_call_target="tpu_custom_call" | custom-call | flops 1073741824 | bytes 6291456 | tf_op jit(solution)/shard_map/pallas_call | solution.py:97
  101.0 1.3 copy-done.1
  102.3 22.1 %all-to-all-done.2 = bf16[4,8,4,32,256]{4,3,2,1,0:T(8,128)(2,1)S(1)} async-done(((bf16[4,8,4,32,256]{4,3,2,1,0:T(8,128)(2,1)}), bf16[4,8,4,32,256]{4,3,2,1,0:T(8,128)(2,1)S(1)}, u32[]{:S(2)}, u32[]{:S(2)}) %all-to-all-start.2) | async-done | bytes 2097184 | tf_op jit(solution)/shard_map/all_to_all | solution.py:28
  124.4 1.6 %copy-done.2 = bf16[1024,1024]{1,0:T(8,128)(2,1)S(1)} copy-done((bf16[1024,1024]{1,0:T(8,128)(2,1)S(1)}, bf16[1024,1024]{1,0:T(8,128)(2,1)}, u32[]{:S(2)}) %copy-start.2) | copy-done | bytes 2097176
  126.0 8.7 %shard_map.51 = (bf16[4,32,256]{2,1,0:T(8,128)(2,1)}, bf16[4,2,256,256]{3,2,1,0:T(8,128)(2,1)}) custom-call(s32[64]{0:T(128)S(1)} %copy-done, bf16[1024,1024]{1,0:T(8,128)(2,1)S(1)} %copy-done.2, bf16[2,1024,256]{2,1,0:T(8,128)(2,1)S(1)} %get-tuple-element.16.others_in, bf16[32,4,32,256]{3,2,1,0:T(8,128)(2,1)S(1)} %bitcast.10), custom_call_target="tpu_custom_call" | custom-call | flops 3221225472 | bytes 6291456 | tf_op jit(solution)/shard_map/pallas_call | solution.py:161
  (17 shorter events, 0.1 us)
Async XLA Ops:
  0.6 36.5 %copy-start.3 = (bf16[4,32,256]{2,1,0:T(8,128)(2,1)S(1)}, bf16[4,32,256]{2,1,0:T(8,128)(2,1)}, u32[]{:S(2)}) copy-start(bf16[4,32,256]{2,1,0:T(8,128)(2,1)} %param.3) | copy-start | bytes 196612
  1.5 26.1 %collective-permute-start = (bf16[2,32,256]{2,1,0:T(8,128)(2,1)S(1)}, bf16[2,32,256]{2,1,0:T(8,128)(2,1)S(1)}, u32[]{:S(2)}, u32[]{:S(2)}) collective-permute-start(bf16[2,32,256]{2,1,0:T(8,128)(2,1)S(1)} %get-tuple-element.24), channel_id=1, source_target_pairs={{0,0},{1,1},{2,32},{3,33},{4,64},{5,65},{6,96},{7,97},{8,128},{9,1... | collective-permute-start | bytes 98312 | tf_op jit(solution)/shard_map/ppermute | solution.py:43
  7.1 20.5 %collective-permute-start.1 = (bf16[2,32,256]{2,1,0:T(8,128)(2,1)S(1)}, bf16[2,32,256]{2,1,0:T(8,128)(2,1)S(1)}, u32[]{:S(2)}, u32[]{:S(2)}) collective-permute-start(bf16[2,32,256]{2,1,0:T(8,128)(2,1)S(1)} %get-tuple-element.25), channel_id=1, source_target_pairs={{0,1},{1,0},{2,33},{3,32},{4,65},{5,64},{6,97},{7,96},{8,129},{9,1... | collective-permute-start | bytes 98312 | tf_op jit(solution)/shard_map/ppermute | solution.py:43
  11.6 25.1 %all-to-all-start = ((bf16[32,2,1024]{2,1,0:T(2,128)(2,1)}), bf16[32,2,1024]{2,1,0:T(2,128)(2,1)S(1)}, u32[]{:S(2)}, u32[]{:S(2)}) async-start(bf16[32,2,1024]{2,1,0:T(2,128)(2,1)} %reshape.12), calls=%async_computation | async-start | bytes 262144 | tf_op jit(solution)/shard_map/all_to_all | solution.py:28
  38.0 28.8 %all-to-all-start.1 = ((bf16[8,4,32,256]{3,2,1,0:T(8,128)(2,1)}), bf16[8,4,32,256]{3,2,1,0:T(8,128)(2,1)S(1)}, u32[]{:S(2)}, u32[]{:S(2)}) async-start(bf16[8,4,32,256]{3,2,1,0:T(8,128)(2,1)} %broadcast_in_dim.12), calls=%async_computation.1 | async-start | bytes 1048576 | tf_op jit(solution)/shard_map/all_to_all | solution.py:28
  41.5 16.3 %collective-permute-start.4 = (bf16[1,64,1536]{2,1,0:T(8,128)(2,1)S(1)}, bf16[1,64,1536]{2,1,0:T(8,128)(2,1)S(1)}, u32[]{:S(2)}, u32[]{:S(2)}) collective-permute-start(bf16[1,64,1536]{2,1,0:T(8,128)(2,1)S(1)} %maximum_bitcast_fusion), channel_id=1, source_target_pairs={{384,0},{448,64},{0,128},{64,192},{128,256},{192,320},{256,384},{3... | collective-permute-start | bytes 589832 | tf_op jit(solution)/shard_map/ppermute | solution.py:184
  47.0 10.7 %collective-permute-start.3 = (bf16[1,64,1536]{2,1,0:T(8,128)(2,1)S(1)}, bf16[1,64,1536]{2,1,0:T(8,128)(2,1)S(1)}, u32[]{:S(2)}, u32[]{:S(2)}) collective-permute-start(bf16[1,64,1536]{2,1,0:T(8,128)(2,1)S(1)} %maximum_bitcast_fusion), channel_id=1, source_target_pairs={{128,0},{192,64},{256,128},{320,192},{384,256},{448,320},{0,384},{... | collective-permute-start | bytes 589832 | tf_op jit(solution)/shard_map/ppermute | solution.py:184
  52.5 14.3 %collective-permute-start.2 = (bf16[1,64,1536]{2,1,0:T(8,128)(2,1)S(1)}, bf16[1,64,1536]{2,1,0:T(8,128)(2,1)S(1)}, u32[]{:S(2)}, u32[]{:S(2)}) collective-permute-start(bf16[1,64,1536]{2,1,0:T(8,128)(2,1)S(1)} %maximum_bitcast_fusion), channel_id=1, source_target_pairs={{256,0},{320,64},{384,128},{448,192},{0,256},{64,320},{128,384},{1... | collective-permute-start | bytes 589832 | tf_op jit(solution)/shard_map/ppermute | solution.py:184
  68.4 21.1 %collective-permute-start.6 = (bf16[2,64,1536]{2,1,0:T(8,128)(2,1)S(1)}, bf16[2,64,1536]{2,1,0:T(8,128)(2,1)S(1)}, u32[]{:S(2)}, u32[]{:S(2)}) collective-permute-start(bf16[2,64,1536]{2,1,0:T(8,128)(2,1)S(1)} %get-tuple-element.18), channel_id=1, source_target_pairs={{448,0},{0,64},{64,128},{128,192},{192,256},{256,320},{320,384},{3... | collective-permute-start | bytes 1179656 | tf_op jit(solution)/shard_map/ppermute | solution.py:184
  77.4 11.4 %collective-permute-start.5 = (bf16[2,64,1536]{2,1,0:T(8,128)(2,1)S(1)}, bf16[2,64,1536]{2,1,0:T(8,128)(2,1)S(1)}, u32[]{:S(2)}, u32[]{:S(2)}) collective-permute-start(bf16[2,64,1536]{2,1,0:T(8,128)(2,1)S(1)} %get-tuple-element.19), channel_id=1, source_target_pairs={{64,0},{128,64},{192,128},{256,192},{320,256},{384,320},{448,384},... | collective-permute-start | bytes 1179656 | tf_op jit(solution)/shard_map/ppermute | solution.py:184
  90.3 7.7 %copy-start = (s32[64]{0:T(128)S(1)}, s32[64]{0:T(128)}, u32[]{:S(2)}) copy-start(s32[64]{0:T(128)} %ranks.3) | copy-start | bytes 772
  90.3 7.7 %collective-permute-start.7 = (bf16[8,64,1536]{2,1,0:T(8,128)(2,1)}, bf16[8,64,1536]{2,1,0:T(8,128)(2,1)}, u32[]{:S(2)}, u32[]{:S(2)}) collective-permute-start(bf16[8,64,1536]{2,1,0:T(8,128)(2,1)} %constant_dynamic-update-slice_fusion.here), channel_id=1, source_target_pairs={{0,32},{32,0},{1,33},{33,1},{2,34},{34,2},{3,35},{35,3},{4,36},{36... | collective-permute-start | bytes 4718600 | tf_op jit(solution)/shard_map/ppermute | solution.py:210
  94.4 30.0 %all-to-all-start.2 = ((bf16[4,8,4,32,256]{4,3,2,1,0:T(8,128)(2,1)}), bf16[4,8,4,32,256]{4,3,2,1,0:T(8,128)(2,1)S(1)}, u32[]{:S(2)}, u32[]{:S(2)}) async-start(bf16[4,8,4,32,256]{4,3,2,1,0:T(8,128)(2,1)} %broadcast_in_dim.15), calls=%async_computation.2 | async-start | bytes 4194304 | tf_op jit(solution)/shard_map/all_to_all | solution.py:28
  101.0 1.3 copy-start.1
  124.4 1.6 %copy-start.2 = (bf16[1024,1024]{1,0:T(8,128)(2,1)S(1)}, bf16[1024,1024]{1,0:T(8,128)(2,1)}, u32[]{:S(2)}) copy-start(bf16[1024,1024]{1,0:T(8,128)(2,1)} %copy-done.1) | copy-start | bytes 6291460
